TPU v7x, 32 devices: a whole 2x2x4 slice. The times are simulated.
32 devices in a mesh: groups: 2 (over y), frame: 4 (over x, core), row: 4 (over z).
Axes of the slice: x: 2, y: 2, z: 4, core: 2. Of those that a mesh axis runs over, the one named last changes fastest.
Arguments:
- observed: float32 [16, 128, 2048], P('frame', ('groups', 'row')), parts along dimension 1, may hold values from 0.5 to 8
- kernels: float32 [8, 5], replicated, may hold values from 0.05 to 1
- band_kernel: int32 [16], P('groups'), parts along dimension 0, may hold values from 0 to 7
- masks: int32 [256, 128, 16], P(None, ('groups', 'row'), 'frame'), parts along dimension 1, may hold values from 0 to 1, as said below
Outputs:
- spikes: bfloat16 [16, 128, 2048], P(None, ('groups', 'row'), 'frame'), parts along dimension 1
- traces: float32 [512, 16], P(('groups', 'frame', 'row')), parts along dimension 0
There are 2 independent parts, one for each index of `groups`. A program takes and returns all parts, laid end to end along the dimension named above; an argument that names none is the same for every part. Nothing has to cross between parts.
Inputs may be any that keep to these rules, and one draw needn't show every extreme that they name: `masks`: each component covers the tile at its centre and a random half of the tiles within 8 rows and one tile column of that centre, so it covers at least one tile.
All inputs are finite; a program needn't handle non-finite values.
Results may differ from a plain program's by a relative error of at most 0.0062.
Values may be sent and summed in bfloat16 or wider, within the bound.
A program may use at most 64 MiB of HBM per device.

v0:
```python
import jax
import jax.numpy as jnp
from jax import lax
from jax.sharding import PartitionSpec as P

TILE = 128
BAND = 8
ITERS = 3
SMOOTHING = 1024.0
DECAY_RATE = 0.9


def padded_2(cells, sides, width):
    for axis, dim in sides:
        count = lax.axis_size(axis)
        ends = count - 1
        head = lax.slice_in_dim(cells, 0, width, axis=dim)
        tail = lax.slice_in_dim(cells, cells.shape[dim] - width, cells.shape[dim], axis=dim)
        cells = jnp.concatenate(
            [
                lax.ppermute(tail, axis, [(i, (i + 1) % count) for i in range(ends)]),
                cells,
                lax.ppermute(head, axis, [((i + 1) % count, i) for i in range(ends)]),
            ],
            axis=dim,
        )
    return cells


def tap_rows(tap_table, band_kernel, first_row, row_count, height):
    row_ids = jnp.clip(first_row + jnp.arange(row_count), 0, height - 1)
    row_bands = row_ids // BAND
    band_slots = jnp.arange(band_kernel.shape[0])
    kernel_ids = jnp.sum(
        jnp.where(row_bands[:, None] == band_slots[None, :], band_kernel[None, :], 0), axis=1
    )
    kernel_slots = jnp.arange(tap_table.shape[0])
    picked = jnp.where(
        kernel_ids[:, None, None] == kernel_slots[None, :, None], tap_table[None, :, :], 0.0
    )
    return jnp.sum(picked, axis=1)


def blur_rows(padded, row_taps, row_count):
    summed = row_taps[:, 0][None, :, None] * padded[:, 0:row_count]
    for offset in range(1, 5):
        summed = (
            summed + row_taps[:, offset][None, :, None] * padded[:, offset : offset + row_count]
        )
    return summed


def back_rows(padded_quotient, outer_taps, row_count):
    summed = outer_taps[4 : 4 + row_count, 0][None, :, None] * padded_quotient[:, 4 : 4 + row_count]
    for offset in range(1, 5):
        start = 4 - offset
        summed = (
            summed
            + outer_taps[start : start + row_count, offset][None, :, None]
            * padded_quotient[:, start : start + row_count]
        )
    return summed


def temporal(series_block):
    frame_total, item_count, columns = series_block.shape
    values = series_block.astype(jnp.float32).reshape(frame_total, item_count * columns)
    frame_ids = jnp.arange(frame_total)
    at_ends = (frame_ids == 0) | (frame_ids == frame_total - 1)
    middle = (1.0 + SMOOTHING * jnp.where(at_ends, 1.0, 2.0)).astype(jnp.float32)
    sub_diag = jnp.where(frame_ids == 0, 0.0, -SMOOTHING).astype(jnp.float32)
    super_diag = jnp.where(frame_ids == frame_total - 1, 0.0, -SMOOTHING).astype(jnp.float32)
    baseline = lax.linalg.tridiagonal_solve(sub_diag, middle, super_diag, values)
    detrended = values - baseline
    earlier = jnp.concatenate(
        [jnp.zeros((1, values.shape[1]), jnp.float32), detrended[:-1]], axis=0
    )
    result = (detrended - DECAY_RATE * earlier).astype(jnp.bfloat16)
    return result.reshape(frame_total, item_count, columns)


def local(observed, kernels, band_kernel, masks):
    frames_dev, rows_dev, row_pixels = observed.shape
    height = rows_dev * lax.axis_size("row")
    tap_table = kernels / jnp.sum(kernels, axis=1, keepdims=True)
    first_row = lax.axis_index("row") * rows_dev
    own_taps = tap_rows(tap_table, band_kernel, first_row, rows_dev, height)
    outer_taps = tap_rows(tap_table, band_kernel, first_row - 2, rows_dev + 4, height)
    current = observed
    for iteration in range(ITERS):
        padded = padded_2(current, (("row", 1),), 2)
        blurred = blur_rows(padded, own_taps, rows_dev)
        quotient = observed / blurred
        padded_quotient = padded_2(quotient, (("row", 1),), 2)
        current = current * back_rows(padded_quotient, outer_taps, rows_dev)
    estimate = current.astype(jnp.bfloat16)
    spikes = temporal(lax.all_to_all(estimate, "frame", split_axis=2, concat_axis=0, tiled=True))
    frames_all, _, columns = spikes.shape
    tile_count = columns // TILE
    tile_sums = jnp.sum(
        spikes.reshape(frames_all, rows_dev * tile_count, TILE).astype(jnp.float32), axis=2
    )
    weights = masks.astype(jnp.float32).reshape(masks.shape[0], rows_dev * tile_count)
    local_sums = lax.dot_general(
        weights, tile_sums, (((1,), (1,)), ((), ())), precision=lax.Precision.HIGHEST
    )
    counts = jnp.sum(weights, axis=1)
    trace_sums, totals = (
        lax.psum_scatter(local_sums, ("frame", "row"), scatter_dimension=0, tiled=True),
        lax.psum_scatter(counts, ("frame", "row"), scatter_dimension=0, tiled=True),
    )
    traces = trace_sums / (TILE * totals[:, None])
    return (spikes, traces)


def solution(mesh):
    in_specs = (
        P("frame", ("groups", "row"), None),
        P(),
        P("groups"),
        P(None, ("groups", "row"), "frame"),
    )
    out_specs = (P(None, ("groups", "row"), "frame"), P(("groups", "frame", "row"), None))
    return jax.shard_map(local, mesh=mesh, in_specs=in_specs, out_specs=out_specs, check_vma=False)
```

profile of v0, /device:TPU:0, one launch (start us, length us, event | category | flops | bytes accessed | tf_op | source)
XLA Modules:
  0.0 222.3 jit_solution(17117470301086755105)
XLA Ops:
  7.2 1.1 fusion.69
  8.4 5.0 %collective-permute-start = (f32[4,2,2048]{2,0,1:T(4,128)S(1)}, f32[4,2,2048]{2,0,1:T(4,128)S(1)}, u32[]{:S(2)}, u32[]{:S(2)}) collective-permute-start(f32[4,2,2048]{2,0,1:T(4,128)S(1)} %copy.150), channel_id=1, source_target_pairs={{0,1},{1,2},{2,3},{4,5},{5,6},{6,7},{8,9},{9,10},{10,11},{12,13},{... | collective-permute-start | bytes 196616 | tf_op jit(solution)/shard_map/ppermute | solution.py:21
  13.4 1.3 collective-permute-start.1
  14.7 0.8 reduce_sum.64
  15.5 0.8 broadcast_divide_fusion.1
  16.3 0.1 copy.106
  16.4 0.7 select_reduce_fusion.2
  17.1 0.1 select_reduce_fusion
  17.2 0.7 select_reduce_fusion.3
  18.0 0.1 select_reduce_fusion.1
  18.1 0.1 slice_bitcast_fusion.24
  18.1 0.9 convert_element_type.45
  19.1 1.5 constant_dynamic-update-slice_fusion
  20.6 0.8 fusion.56
  21.4 1.3 collective-permute-start.2
  22.7 5.2 %collective-permute-start.3 = (f32[4,2,2048]{2,0,1:T(4,128)S(1)}, f32[4,2,2048]{2,0,1:T(4,128)S(1)}, u32[]{:S(2)}, u32[]{:S(2)}) collective-permute-start(f32[4,2,2048]{2,0,1:T(4,128)S(1)} %get-tuple-element.75), channel_id=1, source_target_pairs={{0,1},{1,2},{2,3},{4,5},{5,6},{6,7},{8,9},{9,10},{10,11},{12,13},{... | collective-permute-start | bytes 196616 | tf_op jit(solution)/shard_map/ppermute | solution.py:21
  27.9 0.3 collective-permute-done.2
  28.2 1.6 collective-permute-done.3
  29.8 0.9 fusion.40
  30.7 4.3 %collective-permute-start.4 = (f32[4,2,2048]{2,0,1:T(4,128)S(1)}, f32[4,2,2048]{2,0,1:T(4,128)S(1)}, u32[]{:S(2)}, u32[]{:S(2)}) collective-permute-start(f32[4,2,2048]{2,0,1:T(4,128)S(1)} %get-tuple-element.72), channel_id=1, source_target_pairs={{0,1},{1,2},{2,3},{4,5},{5,6},{6,7},{8,9},{9,10},{10,11},{12,13},{... | collective-permute-start | bytes 196616 | tf_op jit(solution)/shard_map/ppermute | solution.py:21
  34.9 1.3 collective-permute-start.5
  36.2 0.7 fusion.71
  37.0 4.1 %collective-permute-done.5 = f32[4,2,2048]{2,0,1:T(4,128)S(1)} collective-permute-done((f32[4,2,2048]{2,0,1:T(4,128)S(1)}, f32[4,2,2048]{2,0,1:T(4,128)S(1)}, u32[]{:S(2)}, u32[]{:S(2)}) %collective-permute-start.5) | collective-permute-done | bytes 65568 | tf_op jit(solution)/shard_map/ppermute | solution.py:23
  41.1 0.9 fusion.31
  42.0 1.3 collective-permute-start.6
  43.3 4.5 %collective-permute-start.7 = (f32[4,2,2048]{2,0,1:T(4,128)S(1)}, f32[4,2,2048]{2,0,1:T(4,128)S(1)}, u32[]{:S(2)}, u32[]{:S(2)}) collective-permute-start(f32[4,2,2048]{2,0,1:T(4,128)S(1)} %get-tuple-element.71), channel_id=1, source_target_pairs={{0,1},{1,2},{2,3},{4,5},{5,6},{6,7},{8,9},{9,10},{10,11},{12,13},{... | collective-permute-start | bytes 196616 | tf_op jit(solution)/shard_map/ppermute | solution.py:21
  47.9 0.3 collective-permute-done.6
  48.2 1.6 collective-permute-done.7
  49.8 0.6 fusion.22
  50.4 4.3 %collective-permute-start.8 = (f32[4,2,2048]{2,0,1:T(4,128)S(1)}, f32[4,2,2048]{2,0,1:T(4,128)S(1)}, u32[]{:S(2)}, u32[]{:S(2)}) collective-permute-start(f32[4,2,2048]{2,0,1:T(4,128)S(1)} %get-tuple-element.68), channel_id=1, source_target_pairs={{0,1},{1,2},{2,3},{4,5},{5,6},{6,7},{8,9},{9,10},{10,11},{12,13},{... | collective-permute-start | bytes 196616 | tf_op jit(solution)/shard_map/ppermute | solution.py:21
  54.7 1.3 collective-permute-start.9
  56.0 0.7 fusion.72
  58.0 3.5 %collective-permute-done.9 = f32[4,2,2048]{2,0,1:T(4,128)S(1)} collective-permute-done((f32[4,2,2048]{2,0,1:T(4,128)S(1)}, f32[4,2,2048]{2,0,1:T(4,128)S(1)}, u32[]{:S(2)}, u32[]{:S(2)}) %collective-permute-start.9) | collective-permute-done | bytes 65568 | tf_op jit(solution)/shard_map/ppermute | solution.py:23
  61.5 0.9 fusion.13
  62.4 1.3 collective-permute-start.10
  63.7 4.5 %collective-permute-start.11 = (f32[4,2,2048]{2,0,1:T(4,128)S(1)}, f32[4,2,2048]{2,0,1:T(4,128)S(1)}, u32[]{:S(2)}, u32[]{:S(2)}) collective-permute-start(f32[4,2,2048]{2,0,1:T(4,128)S(1)} %get-tuple-element.67), channel_id=1, source_target_pairs={{0,1},{1,2},{2,3},{4,5},{5,6},{6,7},{8,9},{9,10},{10,11},{12,13},{... | collective-permute-start | bytes 196616 | tf_op jit(solution)/shard_map/ppermute | solution.py:21
  68.2 0.3 collective-permute-done.10
  68.5 1.6 collective-permute-done.11
  70.1 0.6 fusion.60
  70.7 1.5 copy.117
  72.2 2.9 %reshape.1472 = bf16[4,2,16384]{2,1,0:T(2,128)(2,1)} reshape(bf16[2048,4,16]{2,1,0:T(4,128)(2,1)S(1)} %bitcast.135) | data formatting | bytes 524288
  75.1 3.4 %all-to-all-start = ((bf16[4,2,16384]{2,1,0:T(2,128)(2,1)}), bf16[4,2,16384]{2,1,0:T(2,128)(2,1)S(1)}, u32[]{:S(2)}, u32[]{:S(2)}) async-start(bf16[4,2,16384]{2,1,0:T(2,128)(2,1)} %reshape.1472), calls=%async_computation | async-start | bytes 524288 | tf_op jit(solution)/shard_map/all_to_all | solution.py:97
  78.6 0.7 fusion.70
  106.8 0.6 dynamic-slice
  108.1 35.6 %all-reduce.1 = f32[256]{0:T(256)S(1)} all-reduce(f32[256]{0:T(256)S(1)} %convert_reduce_fusion), channel_id=3, replica_groups=mesh['groups'=2,'frame'=4,'row'=4] {'frame','row'}, use_global_device_ids=true, to_apply=%region_8.9.clone | all-reduce | flops 256 | bytes 2048
  143.7 1.4 reshape.1473
  145.1 1.1 copy.118
  146.3 0.4 reshape.1467
  146.7 0.2 copy.119
  146.9 0.7 slice_bitcast_fusion
  148.3 0.3 copy.124
  148.6 9.3 %subtract_divide_fusion.1 = (f32[1,8192]{1,0:T(1,128)S(1)}, f32[1,8192]{1,0:T(1,128)S(1)}, f32[1,8192]{1,0:T(1,128)S(1)}, f32[1,8192]{1,0:T(1,128)S(1)}, f32[1,8...) fusion(f32[1,8192]{1,0:T(1,128)S(1)} %bitcast.161, ...), kind=kLoop, calls=%fused_computation.131 | loop fusion | flops 344064 | bytes 950384 | tf_op jit(solution)/shard_map/eval_jaxpr/div | solution.py:73
  157.9 1.0 multiply_subtract_fusion
  158.9 0.8 concatenate.72
  159.7 0.1 convert_bitcast_fusion
  159.8 0.1 copy.142
  159.9 0.2 reduce_sum.68
  160.1 0.1 convolution_bitcast_fusion
  160.3 0.7 copy.122
  161.1 0.1 dynamic-slice_multiply_fusion
  161.1 0.8 copy.141
  161.9 52.1 %reduce-scatter.4.cloned.1.call-done = f32[16,16]{1,0:T(8,128)} async-done(((f32[256,16]{1,0:T(8,128)}), f32[16,16]{1,0:T(8,128)}) %reduce-scatter.4.cloned.1.call-update) | async-done | bytes 1040
  214.0 0.8 copy.123
  214.8 0.7 copy.121
  (50 shorter events, 1.0 us)
Async XLA Ops:
  7.2 13.4 %copy-start = (f32[4,16,2048]{2,1,0:T(8,128)S(1)}, f32[4,16,2048]{2,1,0:T(8,128)}, u32[]{:S(2)}) copy-start(f32[4,16,2048]{2,1,0:T(8,128)} %param.4) | copy-start | bytes 1572868
  8.4 10.7 %collective-permute-start = (f32[4,2,2048]{2,0,1:T(4,128)S(1)}, f32[4,2,2048]{2,0,1:T(4,128)S(1)}, u32[]{:S(2)}, u32[]{:S(2)}) collective-permute-start(f32[4,2,2048]{2,0,1:T(4,128)S(1)} %copy.150), channel_id=1, source_target_pairs={{0,1},{1,2},{2,3},{4,5},{5,6},{6,7},{8,9},{9,10},{10,11},{12,13},{... | collective-permute-start | bytes 196616 | tf_op jit(solution)/shard_map/ppermute | solution.py:21
  13.4 7.2 %collective-permute-start.1 = (f32[4,2,2048]{2,0,1:T(4,128)S(1)}, f32[4,2,2048]{2,0,1:T(4,128)S(1)}, u32[]{:S(2)}, u32[]{:S(2)}) collective-permute-start(f32[4,2,2048]{2,0,1:T(4,128)S(1)} %copy.149), channel_id=1, source_target_pairs={{1,0},{2,1},{3,2},{5,4},{6,5},{7,6},{9,8},{10,9},{11,10},{13,12},{... | collective-permute-start | bytes 196616 | tf_op jit(solution)/shard_map/ppermute | solution.py:23
  21.4 6.8 %collective-permute-start.2 = (f32[4,2,2048]{2,0,1:T(4,128)S(1)}, f32[4,2,2048]{2,0,1:T(4,128)S(1)}, u32[]{:S(2)}, u32[]{:S(2)}) collective-permute-start(f32[4,2,2048]{2,0,1:T(4,128)S(1)} %get-tuple-element.74), channel_id=1, source_target_pairs={{1,0},{2,1},{3,2},{5,4},{6,5},{7,6},{9,8},{10,9},{11,10},{13,12},{... | collective-permute-start | bytes 196616 | tf_op jit(solution)/shard_map/ppermute | solution.py:23
  22.7 7.1 %collective-permute-start.3 = (f32[4,2,2048]{2,0,1:T(4,128)S(1)}, f32[4,2,2048]{2,0,1:T(4,128)S(1)}, u32[]{:S(2)}, u32[]{:S(2)}) collective-permute-start(f32[4,2,2048]{2,0,1:T(4,128)S(1)} %get-tuple-element.75), channel_id=1, source_target_pairs={{0,1},{1,2},{2,3},{4,5},{5,6},{6,7},{8,9},{9,10},{10,11},{12,13},{... | collective-permute-start | bytes 196616 | tf_op jit(solution)/shard_map/ppermute | solution.py:21
  30.7 6.3 %collective-permute-start.4 = (f32[4,2,2048]{2,0,1:T(4,128)S(1)}, f32[4,2,2048]{2,0,1:T(4,128)S(1)}, u32[]{:S(2)}, u32[]{:S(2)}) collective-permute-start(f32[4,2,2048]{2,0,1:T(4,128)S(1)} %get-tuple-element.72), channel_id=1, source_target_pairs={{0,1},{1,2},{2,3},{4,5},{5,6},{6,7},{8,9},{9,10},{10,11},{12,13},{... | collective-permute-start | bytes 196616 | tf_op jit(solution)/shard_map/ppermute | solution.py:21
  34.9 6.2 %collective-permute-start.5 = (f32[4,2,2048]{2,0,1:T(4,128)S(1)}, f32[4,2,2048]{2,0,1:T(4,128)S(1)}, u32[]{:S(2)}, u32[]{:S(2)}) collective-permute-start(f32[4,2,2048]{2,0,1:T(4,128)S(1)} %get-tuple-element.73), channel_id=1, source_target_pairs={{1,0},{2,1},{3,2},{5,4},{6,5},{7,6},{9,8},{10,9},{11,10},{13,12},{... | collective-permute-start | bytes 196616 | tf_op jit(solution)/shard_map/ppermute | solution.py:23
  42.0 6.2 %collective-permute-start.6 = (f32[4,2,2048]{2,0,1:T(4,128)S(1)}, f32[4,2,2048]{2,0,1:T(4,128)S(1)}, u32[]{:S(2)}, u32[]{:S(2)}) collective-permute-start(f32[4,2,2048]{2,0,1:T(4,128)S(1)} %get-tuple-element.70), channel_id=1, source_target_pairs={{1,0},{2,1},{3,2},{5,4},{6,5},{7,6},{9,8},{10,9},{11,10},{13,12},{... | collective-permute-start | bytes 196616 | tf_op jit(solution)/shard_map/ppermute | solution.py:23
  43.3 6.4 %collective-permute-start.7 = (f32[4,2,2048]{2,0,1:T(4,128)S(1)}, f32[4,2,2048]{2,0,1:T(4,128)S(1)}, u32[]{:S(2)}, u32[]{:S(2)}) collective-permute-start(f32[4,2,2048]{2,0,1:T(4,128)S(1)} %get-tuple-element.71), channel_id=1, source_target_pairs={{0,1},{1,2},{2,3},{4,5},{5,6},{6,7},{8,9},{9,10},{10,11},{12,13},{... | collective-permute-start | bytes 196616 | tf_op jit(solution)/shard_map/ppermute | solution.py:21
  50.4 7.6 %collective-permute-start.8 = (f32[4,2,2048]{2,0,1:T(4,128)S(1)}, f32[4,2,2048]{2,0,1:T(4,128)S(1)}, u32[]{:S(2)}, u32[]{:S(2)}) collective-permute-start(f32[4,2,2048]{2,0,1:T(4,128)S(1)} %get-tuple-element.68), channel_id=1, source_target_pairs={{0,1},{1,2},{2,3},{4,5},{5,6},{6,7},{8,9},{9,10},{10,11},{12,13},{... | collective-permute-start | bytes 196616 | tf_op jit(solution)/shard_map/ppermute | solution.py:21
  54.7 6.8 %collective-permute-start.9 = (f32[4,2,2048]{2,0,1:T(4,128)S(1)}, f32[4,2,2048]{2,0,1:T(4,128)S(1)}, u32[]{:S(2)}, u32[]{:S(2)}) collective-permute-start(f32[4,2,2048]{2,0,1:T(4,128)S(1)} %get-tuple-element.69), channel_id=1, source_target_pairs={{1,0},{2,1},{3,2},{5,4},{6,5},{7,6},{9,8},{10,9},{11,10},{13,12},{... | collective-permute-start | bytes 196616 | tf_op jit(solution)/shard_map/ppermute | solution.py:23
  62.4 6.2 %collective-permute-start.10 = (f32[4,2,2048]{2,0,1:T(4,128)S(1)}, f32[4,2,2048]{2,0,1:T(4,128)S(1)}, u32[]{:S(2)}, u32[]{:S(2)}) collective-permute-start(f32[4,2,2048]{2,0,1:T(4,128)S(1)} %get-tuple-element.66), channel_id=1, source_target_pairs={{1,0},{2,1},{3,2},{5,4},{6,5},{7,6},{9,8},{10,9},{11,10},{13,12},{... | collective-permute-start | bytes 196616 | tf_op jit(solution)/shard_map/ppermute | solution.py:23
  63.7 6.4 %collective-permute-start.11 = (f32[4,2,2048]{2,0,1:T(4,128)S(1)}, f32[4,2,2048]{2,0,1:T(4,128)S(1)}, u32[]{:S(2)}, u32[]{:S(2)}) collective-permute-start(f32[4,2,2048]{2,0,1:T(4,128)S(1)} %get-tuple-element.67), channel_id=1, source_target_pairs={{0,1},{1,2},{2,3},{4,5},{5,6},{6,7},{8,9},{9,10},{10,11},{12,13},{... | collective-permute-start | bytes 196616 | tf_op jit(solution)/shard_map/ppermute | solution.py:21
  72.2 34.6 %copy-start.2 = (u32[32]{0:T(128)S(1)}, u32[32]{0:T(128)}, u32[]{:S(2)}) copy-start(u32[32]{0:T(128)} %constant.60) | copy-start | bytes 388
  72.2 35.9 %copy-start.1 = (s32[256,16,4]{0,2,1:T(4,128)S(1)}, s32[256,16,4]{0,2,1:T(4,128)}, u32[]{:S(2)}) copy-start(s32[256,16,4]{0,2,1:T(4,128)} %param.7) | copy-start | bytes 196612
  75.1 68.6 %all-to-all-start = ((bf16[4,2,16384]{2,1,0:T(2,128)(2,1)}), bf16[4,2,16384]{2,1,0:T(2,128)(2,1)S(1)}, u32[]{:S(2)}, u32[]{:S(2)}) async-start(bf16[4,2,16384]{2,1,0:T(2,128)(2,1)} %reshape.1472), calls=%async_computation | async-start | bytes 524288 | tf_op jit(solution)/shard_map/all_to_all | solution.py:97
  78.5 135.5 %reduce-scatter.4.cloned.1.call-start = ((), (), s32[]{:S(2)}) async-start(), calls=%async_computation.2 | async-start | bytes 139264
Sparse Core Ops, SparseCore 0:
  161.2 52.7 reduce-scatter.3
where the time goes:
time: 224 us; the launch traced here: 222 us
  waiting for transfers between devices  65.4 us (29%)
  between operations  44.1 us (20%)
  starting transfers between devices  39 us (17%)
  blocking collectives  35.6 us (16%)
  other arithmetic  20.2 us (9%)
  local copies, waits for them, and re-layouts  18 us (8%)
    unnamed x2, waiting for transfers between devices  52.1 us
    unnamed x1, blocking collectives  35.6 us
    ppermute x6, starting transfers between devices, padded_2(): lax.ppermute(tail, axis, [(i, (i + 1) % count) for i in range(ends)])  27.8 us
    div x1, other arithmetic, temporal(): lax.linalg.tridiagonal_solve(sub_diag, middle, super_diag, values)  9.26 us
    unnamed x34, local copies, waits for them, and re-layouts  8.98 us
    ppermute x6, waiting for transfers between devices, padded_2(): lax.ppermute(head, axis, [((i + 1) % count, i) for i in range(ends)])  8.5 us
    ppermute x6, starting transfers between devices, padded_2(): lax.ppermute(head, axis, [((i + 1) % count, i) for i in range(ends)])  7.75 us
    ppermute x6, waiting for transfers between devices, padded_2(): lax.ppermute(tail, axis, [(i, (i + 1) % count) for i in range(ends)])  4.75 us
  transfers between devices with their start and end apart: 14, of which 9 were waited for; matrix products, arithmetic and copies ran while one was open for 4% of the time, Pallas kernels for 0%

commit v1 on v0

--- a/solution.py
+++ b/solution.py
@@ -94,7 +94,16 @@
         padded_quotient = padded_2(quotient, (("row", 1),), 2)
         current = current * back_rows(padded_quotient, outer_taps, rows_dev)
     estimate = current.astype(jnp.bfloat16)
-    spikes = temporal(lax.all_to_all(estimate, "frame", split_axis=2, concat_axis=0, tiled=True))
+    step_on_sector_in = lambda array_in, dim_k, array_axis: jnp.concatenate(
+        lax.all_to_all(
+            jnp.stack(jnp.split(array_in, lax.axis_size("frame"), dim_k), axis=0),
+            axis_name="frame",
+            split_axis=0,
+            concat_axis=0,
+        ),
+        array_axis,
+    )
+    spikes = temporal(step_on_sector_in(estimate, 2, 0))
     frames_all, _, columns = spikes.shape
     tile_count = columns // TILE
     tile_sums = jnp.sum(

time: 224 us -> 213 us (0.951)
  waiting for transfers between devices: 65.4 us -> 72.8 us
  local copies, waits for them, and re-layouts: 18 us -> 10.8 us
  other arithmetic: 20.2 us -> 15.3 us
  blocking collectives: 35.6 us -> 31.2 us
    ppermute x6, waiting for transfers between devices: 8.5 us -> 16.3 us  [padded_2(): lax.ppermute(head, axis, [((i + 1) % count, i) for i in range(ends)])]
    unnamed x1, blocking collectives: 35.6 us -> 31.2 us
    unnamed x34, local copies, waits for them, and re-layouts: 8.98 us -> 6.32 us
  transfers between devices with their start and end apart: 14 -> 14, of which waited for: 9 -> 9; matrix products, arithmetic and copies ran while one was open for 4% -> 3% of each run, Pallas kernels for 0% -> 0%
where the time goes in v1:
time: 213 us; the launch traced here: 212 us
  waiting for transfers between devices  72.8 us (34%)
  between operations  44 us (21%)
  starting transfers between devices  37.3 us (18%)
  blocking collectives  31.2 us (15%)
  other arithmetic  15.3 us (7%)
  local copies, waits for them, and re-layouts  10.8 us (5%)
    unnamed x2, waiting for transfers between devices  53.6 us
    unnamed x1, blocking collectives  31.2 us
    ppermute x6, starting transfers between devices, padded_2(): lax.ppermute(tail, axis, [(i, (i + 1) % count) for i in range(ends)])  25.9 us
    ppermute x6, waiting for transfers between devices, padded_2(): lax.ppermute(head, axis, [((i + 1) % count, i) for i in range(ends)])  16.3 us
    div x1, other arithmetic, temporal(): lax.linalg.tridiagonal_solve(sub_diag, middle, super_diag, values)  9.24 us
    ppermute x6, starting transfers between devices, padded_2(): lax.ppermute(head, axis, [((i + 1) % count, i) for i in range(ends)])  7.88 us
    unnamed x34, local copies, waits for them, and re-layouts  6.32 us
  transfers between devices with their start and end apart: 14, of which 9 were waited for; matrix products, arithmetic and copies ran while one was open for 3% of the time, Pallas kernels for 0%

profile of v1, /device:TPU:0, one launch (start us, length us, event | category | flops | bytes accessed | tf_op | source)
XLA Modules:
  0.0 211.6 jit_solution(723358336214308564)
XLA Ops:
  7.2 1.1 fusion.72
  8.2 5.0 %collective-permute-start = (f32[4,2,2048]{2,1,0:T(2,128)S(1)}, f32[4,2,2048]{2,1,0:T(2,128)S(1)}, u32[]{:S(2)}, u32[]{:S(2)}) collective-permute-start(f32[4,2,2048]{2,1,0:T(2,128)S(1)} %get-tuple-element.67), channel_id=1, source_target_pairs={{0,1},{1,2},{2,3},{4,5},{5,6},{6,7},{8,9},{9,10},{10,11},{12,13},{... | collective-permute-start | bytes 196616 | tf_op jit(solution)/shard_map/ppermute | solution.py:21
  13.2 1.4 collective-permute-start.1
  14.7 1.1 constant_dynamic-update-slice_fusion.1
  15.8 0.1 reduce_sum.64
  15.9 0.1 broadcast_divide_fusion.1
  16.0 0.1 copy.8
  16.1 0.1 select_reduce_fusion.2
  16.2 0.1 select_reduce_fusion
  16.3 0.1 select_reduce_fusion.3
  16.4 0.1 select_reduce_fusion.1
  16.5 0.1 slice_bitcast_fusion.28
  16.6 0.0 copy-done.1
  16.7 2.9 %collective-permute-done.1 = f32[4,2,2048]{2,1,0:T(2,128)S(1)} collective-permute-done((f32[4,2,2048]{2,1,0:T(2,128)S(1)}, f32[4,2,2048]{2,1,0:T(2,128)S(1)}, u32[]{:S(2)}, u32[]{:S(2)}) %collective-permute-start.1) | collective-permute-done | bytes 65568 | tf_op jit(solution)/shard_map/ppermute | solution.py:23
  19.6 0.4 fusion.52
  20.0 3.5 %collective-permute-start.3 = (f32[4,2,2048]{2,1,0:T(2,128)S(1)}, f32[4,2,2048]{2,1,0:T(2,128)S(1)}, u32[]{:S(2)}, u32[]{:S(2)}) collective-permute-start(f32[4,2,2048]{2,1,0:T(2,128)S(1)} %get-tuple-element.65), channel_id=1, source_target_pairs={{0,1},{1,2},{2,3},{4,5},{5,6},{6,7},{8,9},{9,10},{10,11},{12,13},{... | collective-permute-start | bytes 196616 | tf_op jit(solution)/shard_map/ppermute | solution.py:21
  23.5 1.3 collective-permute-start.2
  24.8 0.6 collective-permute-done.3
  25.4 4.3 %collective-permute-done.2 = f32[4,2,2048]{2,1,0:T(2,128)S(1)} collective-permute-done((f32[4,2,2048]{2,1,0:T(2,128)S(1)}, f32[4,2,2048]{2,1,0:T(2,128)S(1)}, u32[]{:S(2)}, u32[]{:S(2)}) %collective-permute-start.2) | collective-permute-done | bytes 65568 | tf_op jit(solution)/shard_map/ppermute | solution.py:23
  29.7 0.4 fusion.41
  30.2 1.3 collective-permute-start.5
  31.5 4.5 %collective-permute-start.4 = (f32[4,2,2048]{2,1,0:T(2,128)S(1)}, f32[4,2,2048]{2,1,0:T(2,128)S(1)}, u32[]{:S(2)}, u32[]{:S(2)}) collective-permute-start(f32[4,2,2048]{2,1,0:T(2,128)S(1)} %get-tuple-element.62), channel_id=1, source_target_pairs={{0,1},{1,2},{2,3},{4,5},{5,6},{6,7},{8,9},{9,10},{10,11},{12,13},{... | collective-permute-start | bytes 196616 | tf_op jit(solution)/shard_map/ppermute | solution.py:21
  36.0 0.7 fusion.74
  36.8 1.2 collective-permute-done.4
  37.9 0.5 fusion.32
  38.4 4.3 %collective-permute-start.7 = (f32[4,2,2048]{2,1,0:T(2,128)S(1)}, f32[4,2,2048]{2,1,0:T(2,128)S(1)}, u32[]{:S(2)}, u32[]{:S(2)}) collective-permute-start(f32[4,2,2048]{2,1,0:T(2,128)S(1)} %get-tuple-element.61), channel_id=1, source_target_pairs={{0,1},{1,2},{2,3},{4,5},{5,6},{6,7},{8,9},{9,10},{10,11},{12,13},{... | collective-permute-start | bytes 196616 | tf_op jit(solution)/shard_map/ppermute | solution.py:21
  42.7 1.3 collective-permute-start.6
  44.0 0.6 collective-permute-done.7
  44.6 4.9 %collective-permute-done.6 = f32[4,2,2048]{2,1,0:T(2,128)S(1)} collective-permute-done((f32[4,2,2048]{2,1,0:T(2,128)S(1)}, f32[4,2,2048]{2,1,0:T(2,128)S(1)}, u32[]{:S(2)}, u32[]{:S(2)}) %collective-permute-start.6) | collective-permute-done | bytes 65568 | tf_op jit(solution)/shard_map/ppermute | solution.py:23
  49.5 0.4 fusion.23
  50.0 1.3 collective-permute-start.9
  51.3 4.5 %collective-permute-start.8 = (f32[4,2,2048]{2,1,0:T(2,128)S(1)}, f32[4,2,2048]{2,1,0:T(2,128)S(1)}, u32[]{:S(2)}, u32[]{:S(2)}) collective-permute-start(f32[4,2,2048]{2,1,0:T(2,128)S(1)} %get-tuple-element.58), channel_id=1, source_target_pairs={{0,1},{1,2},{2,3},{4,5},{5,6},{6,7},{8,9},{9,10},{10,11},{12,13},{... | collective-permute-start | bytes 196616 | tf_op jit(solution)/shard_map/ppermute | solution.py:21
  55.8 0.7 fusion.75
  57.9 0.4 fusion.14
  58.4 4.1 %collective-permute-start.11 = (f32[4,2,2048]{2,1,0:T(2,128)S(1)}, f32[4,2,2048]{2,1,0:T(2,128)S(1)}, u32[]{:S(2)}, u32[]{:S(2)}) collective-permute-start(f32[4,2,2048]{2,1,0:T(2,128)S(1)} %get-tuple-element.57), channel_id=1, source_target_pairs={{0,1},{1,2},{2,3},{4,5},{5,6},{6,7},{8,9},{9,10},{10,11},{12,13},{... | collective-permute-start | bytes 196616 | tf_op jit(solution)/shard_map/ppermute | solution.py:21
  62.5 1.3 collective-permute-start.10
  63.8 0.6 collective-permute-done.11
  64.4 4.3 %collective-permute-done.10 = f32[4,2,2048]{2,1,0:T(2,128)S(1)} collective-permute-done((f32[4,2,2048]{2,1,0:T(2,128)S(1)}, f32[4,2,2048]{2,1,0:T(2,128)S(1)}, u32[]{:S(2)}, u32[]{:S(2)}) %collective-permute-start.10) | collective-permute-done | bytes 65568 | tf_op jit(solution)/shard_map/ppermute | solution.py:23
  68.7 0.4 fusion.5
  69.1 0.7 pad_maximum_fusion.11
  69.9 3.4 %all-to-all-start = ((bf16[4,4,16,512]{3,2,1,0:T(8,128)(2,1)}), bf16[4,4,16,512]{3,2,1,0:T(8,128)(2,1)S(1)}, u32[]{:S(2)}, u32[]{:S(2)}) async-start(bf16[4,4,16,512]{3,2,1,0:T(8,128)(2,1)} %pad_maximum_fusion.11), calls=%async_computation | async-start | bytes 524288 | tf_op jit(solution)/shard_map/all_to_all | solution.py:98
  73.3 0.0 reduce-scatter.4.cloned.1.call-start
  73.3 0.7 fusion.73
  101.6 0.6 copy-done.4
  102.2 0.6 dynamic-slice
  103.5 31.2 %all-reduce.1 = f32[256]{0:T(256)S(1)} all-reduce(f32[256]{0:T(256)S(1)} %convert_reduce_fusion), channel_id=3, replica_groups=mesh['groups'=2,'frame'=4,'row'=4] {'frame','row'}, use_global_device_ids=true, to_apply=%region_8.9.clone | all-reduce | flops 256 | bytes 2048
  134.7 0.1 convert_element_type.36
  134.8 0.3 copy.13
  135.1 0.7 slice_bitcast_fusion.4
  136.4 9.2 %subtract_divide_fusion.1 = (f32[1,8192]{1,0:T(1,128)S(1)}, f32[1,8192]{1,0:T(1,128)S(1)}, f32[1,8192]{1,0:T(1,128)S(1)}, f32[1,8192]{1,0:T(1,128)S(1)}, f32[1,8...) fusion(f32[1,8192]{1,0:T(1,128)S(1)} %bitcast.150, ...), kind=kLoop, calls=%fused_computation.140 | loop fusion | flops 344064 | bytes 950384 | tf_op jit(solution)/shard_map/eval_jaxpr/div | solution.py:73
  145.7 0.9 multiply_subtract_fusion
  146.6 0.8 concatenate.72
  147.4 0.1 sub.1744
  147.5 0.1 convert_bitcast_fusion
  147.6 0.1 copy.31
  147.7 0.2 reduce_sum.68
  147.9 0.1 convolution_bitcast_fusion
  148.1 0.7 copy.11
  148.8 0.0 reduce-scatter.4.cloned.1.call-update
  148.8 0.1 dynamic-slice_multiply_fusion
  148.9 0.8 copy.30
  149.7 53.6 %reduce-scatter.4.cloned.1.call-done = f32[16,16]{1,0:T(8,128)} async-done(((f32[256,16]{1,0:T(8,128)}), f32[16,16]{1,0:T(8,128)}) %reduce-scatter.4.cloned.1.call-update) | async-done | bytes 1040
  203.3 0.8 copy.12
  204.1 0.7 copy.10
  (48 shorter events, 1.0 us)
Async XLA Ops:
  8.2 11.3 %collective-permute-start = (f32[4,2,2048]{2,1,0:T(2,128)S(1)}, f32[4,2,2048]{2,1,0:T(2,128)S(1)}, u32[]{:S(2)}, u32[]{:S(2)}) collective-permute-start(f32[4,2,2048]{2,1,0:T(2,128)S(1)} %get-tuple-element.67), channel_id=1, source_target_pairs={{0,1},{1,2},{2,3},{4,5},{5,6},{6,7},{8,9},{9,10},{10,11},{12,13},{... | collective-permute-start | bytes 196616 | tf_op jit(solution)/shard_map/ppermute | solution.py:21
  13.2 6.3 %copy-start = (f32[4,16,2048]{2,1,0:T(8,128)S(1)}, f32[4,16,2048]{2,1,0:T(8,128)}, u32[]{:S(2)}) copy-start(f32[4,16,2048]{2,1,0:T(8,128)} %param.4) | copy-start | bytes 1572868
  13.2 6.3 %collective-permute-start.1 = (f32[4,2,2048]{2,1,0:T(2,128)S(1)}, f32[4,2,2048]{2,1,0:T(2,128)S(1)}, u32[]{:S(2)}, u32[]{:S(2)}) collective-permute-start(f32[4,2,2048]{2,1,0:T(2,128)S(1)} %get-tuple-element.66), channel_id=1, source_target_pairs={{1,0},{2,1},{3,2},{5,4},{6,5},{7,6},{9,8},{10,9},{11,10},{13,12},{... | collective-permute-start | bytes 196616 | tf_op jit(solution)/shard_map/ppermute | solution.py:23
  14.7 1.1 copy-start.2
  14.7 1.4 copy-start.3
  15.8 0.8 copy-start.1
  20.0 5.4 %collective-permute-start.3 = (f32[4,2,2048]{2,1,0:T(2,128)S(1)}, f32[4,2,2048]{2,1,0:T(2,128)S(1)}, u32[]{:S(2)}, u32[]{:S(2)}) collective-permute-start(f32[4,2,2048]{2,1,0:T(2,128)S(1)} %get-tuple-element.65), channel_id=1, source_target_pairs={{0,1},{1,2},{2,3},{4,5},{5,6},{6,7},{8,9},{9,10},{10,11},{12,13},{... | collective-permute-start | bytes 196616 | tf_op jit(solution)/shard_map/ppermute | solution.py:21
  23.5 6.2 %collective-permute-start.2 = (f32[4,2,2048]{2,1,0:T(2,128)S(1)}, f32[4,2,2048]{2,1,0:T(2,128)S(1)}, u32[]{:S(2)}, u32[]{:S(2)}) collective-permute-start(f32[4,2,2048]{2,1,0:T(2,128)S(1)} %get-tuple-element.64), channel_id=1, source_target_pairs={{1,0},{2,1},{3,2},{5,4},{6,5},{7,6},{9,8},{10,9},{11,10},{13,12},{... | collective-permute-start | bytes 196616 | tf_op jit(solution)/shard_map/ppermute | solution.py:23
  30.2 6.6 %collective-permute-start.5 = (f32[4,2,2048]{2,1,0:T(2,128)S(1)}, f32[4,2,2048]{2,1,0:T(2,128)S(1)}, u32[]{:S(2)}, u32[]{:S(2)}) collective-permute-start(f32[4,2,2048]{2,1,0:T(2,128)S(1)} %get-tuple-element.63), channel_id=1, source_target_pairs={{1,0},{2,1},{3,2},{5,4},{6,5},{7,6},{9,8},{10,9},{11,10},{13,12},{... | collective-permute-start | bytes 196616 | tf_op jit(solution)/shard_map/ppermute | solution.py:23
  31.5 6.4 %collective-permute-start.4 = (f32[4,2,2048]{2,1,0:T(2,128)S(1)}, f32[4,2,2048]{2,1,0:T(2,128)S(1)}, u32[]{:S(2)}, u32[]{:S(2)}) collective-permute-start(f32[4,2,2048]{2,1,0:T(2,128)S(1)} %get-tuple-element.62), channel_id=1, source_target_pairs={{0,1},{1,2},{2,3},{4,5},{5,6},{6,7},{8,9},{9,10},{10,11},{12,13},{... | collective-permute-start | bytes 196616 | tf_op jit(solution)/shard_map/ppermute | solution.py:21
  38.4 6.2 %collective-permute-start.7 = (f32[4,2,2048]{2,1,0:T(2,128)S(1)}, f32[4,2,2048]{2,1,0:T(2,128)S(1)}, u32[]{:S(2)}, u32[]{:S(2)}) collective-permute-start(f32[4,2,2048]{2,1,0:T(2,128)S(1)} %get-tuple-element.61), channel_id=1, source_target_pairs={{0,1},{1,2},{2,3},{4,5},{5,6},{6,7},{8,9},{9,10},{10,11},{12,13},{... | collective-permute-start | bytes 196616 | tf_op jit(solution)/shard_map/ppermute | solution.py:21
  42.7 6.8 %collective-permute-start.6 = (f32[4,2,2048]{2,1,0:T(2,128)S(1)}, f32[4,2,2048]{2,1,0:T(2,128)S(1)}, u32[]{:S(2)}, u32[]{:S(2)}) collective-permute-start(f32[4,2,2048]{2,1,0:T(2,128)S(1)} %get-tuple-element.60), channel_id=1, source_target_pairs={{1,0},{2,1},{3,2},{5,4},{6,5},{7,6},{9,8},{10,9},{11,10},{13,12},{... | collective-permute-start | bytes 196616 | tf_op jit(solution)/shard_map/ppermute | solution.py:23
  50.0 7.9 %collective-permute-start.9 = (f32[4,2,2048]{2,1,0:T(2,128)S(1)}, f32[4,2,2048]{2,1,0:T(2,128)S(1)}, u32[]{:S(2)}, u32[]{:S(2)}) collective-permute-start(f32[4,2,2048]{2,1,0:T(2,128)S(1)} %get-tuple-element.59), channel_id=1, source_target_pairs={{1,0},{2,1},{3,2},{5,4},{6,5},{7,6},{9,8},{10,9},{11,10},{13,12},{... | collective-permute-start | bytes 196616 | tf_op jit(solution)/shard_map/ppermute | solution.py:23
  51.3 6.6 %collective-permute-start.8 = (f32[4,2,2048]{2,1,0:T(2,128)S(1)}, f32[4,2,2048]{2,1,0:T(2,128)S(1)}, u32[]{:S(2)}, u32[]{:S(2)}) collective-permute-start(f32[4,2,2048]{2,1,0:T(2,128)S(1)} %get-tuple-element.58), channel_id=1, source_target_pairs={{0,1},{1,2},{2,3},{4,5},{5,6},{6,7},{8,9},{9,10},{10,11},{12,13},{... | collective-permute-start | bytes 196616 | tf_op jit(solution)/shard_map/ppermute | solution.py:21
  58.4 6.0 %collective-permute-start.11 = (f32[4,2,2048]{2,1,0:T(2,128)S(1)}, f32[4,2,2048]{2,1,0:T(2,128)S(1)}, u32[]{:S(2)}, u32[]{:S(2)}) collective-permute-start(f32[4,2,2048]{2,1,0:T(2,128)S(1)} %get-tuple-element.57), channel_id=1, source_target_pairs={{0,1},{1,2},{2,3},{4,5},{5,6},{6,7},{8,9},{9,10},{10,11},{12,13},{... | collective-permute-start | bytes 196616 | tf_op jit(solution)/shard_map/ppermute | solution.py:21
  62.5 6.2 %collective-permute-start.10 = (f32[4,2,2048]{2,1,0:T(2,128)S(1)}, f32[4,2,2048]{2,1,0:T(2,128)S(1)}, u32[]{:S(2)}, u32[]{:S(2)}) collective-permute-start(f32[4,2,2048]{2,1,0:T(2,128)S(1)} %get-tuple-element.56), channel_id=1, source_target_pairs={{1,0},{2,1},{3,2},{5,4},{6,5},{7,6},{9,8},{10,9},{11,10},{13,12},{... | collective-permute-start | bytes 196616 | tf_op jit(solution)/shard_map/ppermute | solution.py:23
  69.9 64.8 %all-to-all-start = ((bf16[4,4,16,512]{3,2,1,0:T(8,128)(2,1)}), bf16[4,4,16,512]{3,2,1,0:T(8,128)(2,1)S(1)}, u32[]{:S(2)}, u32[]{:S(2)}) async-start(bf16[4,4,16,512]{3,2,1,0:T(8,128)(2,1)} %pad_maximum_fusion.11), calls=%async_computation | async-start | bytes 524288 | tf_op jit(solution)/shard_map/all_to_all | solution.py:98
  73.3 130.0 %reduce-scatter.4.cloned.1.call-start = ((), (), s32[]{:S(2)}) async-start(), calls=%async_computation.2 | async-start | bytes 139264
  101.5 0.7 copy-start.4
Sparse Core Ops, SparseCore 0:
  148.9 54.3 reduce-scatter.3
